TPU v7x, 512 devices: a whole 4x4x16 slice. The times are simulated.
512 devices in a mesh: row: 32 (over z, core), col: 16 (over x, y).
Axes of the slice: x: 4, y: 4, z: 16, core: 2. Of those that a mesh axis runs over, the one named last changes fastest.
Arguments:
- x_points: bfloat16 [131072, 256], P(('row', 'col')), may hold values from -1.5 to 1.5
- y_points: bfloat16 [131072, 256], P(('row', 'col')), may hold values from -1.5 to 1.5
- log_a: float32 [131072], P(('row', 'col')), may hold values from -1.5 to 1.5
- log_b: float32 [131072], P(('row', 'col')), may hold values from -1.5 to 1.5
- g_init: float32 [131072], P(('row', 'col')), may hold values from -3 to 3
- tile_list: int32 [24576, 2], P(('row', 'col')), may hold values from 0 to 1023, as said below
- tile_count: int32 [512], P(('row', 'col')), may hold values from 2 to 48, as said below
Outputs:
- f_out: float32 [131072], P(('row', 'col'))
- g_out: float32 [131072], P(('row', 'col'))
Inputs may be any that keep to these rules, and one draw needn't show every extreme that they name: `tile_list`: slots 48 * d to 48 * (d + 1) - 1 belong to device d = row index * 16 + col index. Each slot names a source block held by a device of d's row group and a target block held by a device of d's col group; the slots of one device are distinct pairs. Every block of either cloud is in some active tile. `tile_count`: some device has all 48 slots active.
All inputs are finite; a program needn't handle non-finite values.
Results may differ from a plain program's by a relative error of at most 0.0003.
Values may be sent and summed in bfloat16 or wider, within the bound.
A program may use at most 64 MiB of HBM per device.

v0:
```python
import math

import jax
import jax.numpy as jnp
from jax import lax
from jax.sharding import PartitionSpec as P

BLOCK = 128
ITERS = 2


EPSILON = 0.25
NEGATIVE = -1e30


def block_costs(x_blocks, x_square, y_blocks, y_square, rows, cols):
    x_take = jnp.take(x_blocks, rows, axis=0)
    y_take = jnp.take(y_blocks, cols, axis=0)
    inner = jnp.einsum("tpd,tqd->tpq", x_take, y_take, preferred_element_type=jnp.float32)
    return (
        0.5 * jnp.take(x_square, rows, axis=0)[:, :, None]
        + 0.5 * jnp.take(y_square, cols, axis=0)[:, None, :]
        - inner
    )


def local_max(score_of, targets, shape_blocks, turns):

    def visit(turn_index, acc):
        return acc.at[targets[turn_index]].max(jnp.max(score_of(turn_index), axis=-1))

    return lax.fori_loop(0, turns, visit, jnp.full(shape_blocks, NEGATIVE, jnp.float32))


def local_sum(score_of, targets, top, turns):

    def visit(turn_index, acc):
        rows = targets[turn_index]
        shift = jnp.take(top, rows, axis=0)[:, :, None]
        return acc.at[rows].add(jnp.sum(jnp.exp(score_of(turn_index) - shift), axis=-1))

    return lax.fori_loop(0, turns, visit, jnp.zeros(top.shape, jnp.float32))


def row_potential(score_of, targets, shape_blocks, turns):
    top = lax.pmax(local_max(score_of, targets, shape_blocks, turns), "col")
    total = lax.psum(local_sum(score_of, targets, top, turns), "col")
    return -EPSILON * (top + jnp.log(total))


def col_potential(score_of, targets, shape_blocks, turns):
    top = lax.pmax(
        local_max(score_of, targets, shape_blocks, turns).astype(jnp.bfloat16), "row"
    ).astype(jnp.float32)
    total = lax.psum(local_sum(score_of, targets, top, turns), "row")
    return -EPSILON * (top + jnp.log(total))


def body(x_points, y_points, log_a, log_b, g_init, tile_list, tile_count):
    width = x_points.shape[1]
    points_here = x_points.shape[0]
    per_device = points_here // BLOCK
    row_index = lax.axis_index("row")
    col_index = lax.axis_index("col")
    col_count = lax.axis_size("col")
    x_all = lax.all_gather(x_points, "col", axis=0, tiled=True)
    a_all = lax.all_gather(log_a, "col", axis=0, tiled=True)
    y_all = lax.all_gather(y_points, "row", axis=0, tiled=True)
    y_extra = lax.all_gather(jnp.stack([log_b, g_init]), "row", axis=1, tiled=True)
    x_blocks = x_all.reshape(-1, BLOCK, width)
    y_blocks = y_all.reshape(-1, BLOCK, width)
    x_square = jnp.einsum("bpd,bpd->bp", x_blocks, x_blocks, preferred_element_type=jnp.float32)
    y_square = jnp.einsum("bpd,bpd->bp", y_blocks, y_blocks, preferred_element_type=jnp.float32)
    a_blocks = a_all.reshape(-1, BLOCK)
    b_blocks = y_extra[0].reshape(-1, BLOCK)
    g_blocks = y_extra[1].reshape(-1, BLOCK)
    tiles_here = tile_list.shape[0]
    batch = math.gcd(tiles_here, 8)
    turns = tiles_here // batch
    row_ids = (tile_list[:, 0] - row_index * (col_count * per_device)).reshape(turns, batch)
    col_global = tile_list[:, 1]
    col_ids = (
        col_global // per_device // col_count * per_device + col_global % per_device
    ).reshape(turns, batch)
    active = (jnp.arange(tiles_here, dtype=jnp.int32) < tile_count[0]).reshape(turns, batch)

    def costs_at(turn_index):
        return block_costs(
            x_blocks, x_square, y_blocks, y_square, row_ids[turn_index], col_ids[turn_index]
        )

    f_blocks = jnp.zeros_like(a_blocks)
    for iteration in range(ITERS):

        def f_scores(turn_index):
            cols = col_ids[turn_index]
            scores = (
                jnp.take(g_blocks, cols, axis=0)[:, None, :] - costs_at(turn_index)
            ) / EPSILON + jnp.take(b_blocks, cols, axis=0)[:, None, :]
            return jnp.where(active[turn_index][:, None, None], scores, NEGATIVE)

        f_blocks = row_potential(f_scores, row_ids, a_blocks.shape, turns)

        def g_scores(turn_index):
            rows = row_ids[turn_index]
            scores = (
                jnp.take(f_blocks, rows, axis=0)[:, :, None] - costs_at(turn_index)
            ) / EPSILON + jnp.take(a_blocks, rows, axis=0)[:, :, None]
            scores = jnp.transpose(scores, (0, 2, 1))
            return jnp.where(active[turn_index][:, None, None], scores, NEGATIVE)

        g_blocks = col_potential(g_scores, col_ids, b_blocks.shape, turns)
    f_out = lax.dynamic_slice_in_dim(f_blocks.reshape(-1), col_index * points_here, points_here)
    g_out = lax.dynamic_slice_in_dim(g_blocks.reshape(-1), row_index * points_here, points_here)
    return (f_out, g_out)


def solution(mesh):
    in_specs = (
        P(("row", "col"), None),
        P(("row", "col"), None),
        P(("row", "col")),
        P(("row", "col")),
        P(("row", "col")),
        P(("row", "col"), None),
        P(("row", "col")),
    )
    out_specs = (P(("row", "col")), P(("row", "col")))
    return jax.shard_map(body, mesh=mesh, in_specs=in_specs, out_specs=out_specs, check_vma=False)
```

profile of v0, /device:TPU:1, one launch (start us, length us, event | category | flops | bytes accessed | tf_op | source)
XLA Modules:
  0.0 1156.1 jit_solution(3154675278406226549)
XLA Ops:
  10.2 19.6 %all-gather = f32[16,1,256]{2,1,0:T(1,128)S(1)} all-gather(f32[1,1,256]{2,1,0:T(1,128)} %bitcast.181), channel_id=1, replica_groups=mesh['row'=32,'col'=16] {'col'}, dimensions={0}, use_global_device_ids=true | all-gather | bytes 17408 | tf_op jit(solution)/shard_map/all_gather | solution.py:67
  30.5 41.8 %all_gather.12 = f32[2,8192]{1,0:T(2,128)S(1)} all-gather(f32[2,256]{1,0:T(2,128)S(1)} %pad_maximum_fusion), channel_id=1, replica_groups=mesh['row'=32,'col'=16] {'row'}, dimensions={1}, use_global_device_ids=true | all-gather | bytes 67584 | tf_op jit(solution)/shard_map/all_gather | solution.py:69
  77.3 74.6 %all-gather.6.cloned.1.call-done = bf16[8192,256]{1,0:T(8,128)(2,1)} async-done(((bf16[256,256]{1,0:T(8,128)(2,1)}), bf16[8192,256]{1,0:T(8,128)(2,1)}) %all-gather.6.cloned.1.call-update) | async-done | bytes 4194320 | tf_op jit(solution)/shard_map/all_gather | solution.py:68
  151.9 3.3 fusion.112
  155.2 42.2 %while.104 = (s32[]{:T(128)}, f32[32,128]{1,0:T(8,128)S(1)}, s32[6,8]{1,0:T(8,128)S(1)}, pred[6,8]{1,0:T(8,128)(4,1)S(1)}, s32[6,8]{1,0:T(8,128)S(1)}, /*index=5...) while((s32[]{:T(128)}, f32[32,128]{1,0:T(8,128)S(1)}, ...), condition=%wide.region_3.8_spmd, body=%wide.region_0.7_spmd.sunk | while | flops 68558968 | bytes 3252905 | solution.py:32
  197.5 60.4 %pmax.28 = f32[32,128]{1,0:T(8,128)S(1)} all-reduce(f32[32,128]{1,0:T(8,128)S(1)} %get-tuple-element.1538), channel_id=1, replica_groups=mesh['row'=32,'col'=16] {'col'}, use_global_device_ids=true, to_apply=%region_4.9 | all-reduce | flops 4096 | bytes 32768 | tf_op jit(solution)/shard_map/pmax | solution.py:46
  257.9 45.7 %while.105 = (s32[]{:T(128)}, f32[32,128]{1,0:T(8,128)S(1)}, s32[6,8]{1,0:T(8,128)S(1)}, pred[6,8]{1,0:T(8,128)(4,1)S(1)}, s32[6,8]{1,0:T(8,128)S(1)}, /*index=5...) while((s32[]{:T(128)}, f32[32,128]{1,0:T(8,128)S(1)}, ...), condition=%wide.region_8.13_spmd, body=%wide.region_5.12_spmd.sunk | while | flops 68691064 | bytes 3273425 | solution.py:42
  303.6 56.0 %psum.28 = f32[32,128]{1,0:T(8,128)S(1)} all-reduce(f32[32,128]{1,0:T(8,128)S(1)} %get-tuple-element.1539), channel_id=1, replica_groups=mesh['row'=32,'col'=16] {'col'}, use_global_device_ids=true, to_apply=%region_9.14 | all-reduce | flops 4096 | bytes 32768 | tf_op jit(solution)/shard_map/psum | solution.py:47
  359.6 42.5 %while.106 = (s32[]{:T(128)}, f32[64,128]{1,0:T(8,128)S(1)}, s32[6,8]{1,0:T(8,128)S(1)}, pred[6,8]{1,0:T(8,128)(4,1)S(1)}, s32[6,8]{1,0:T(8,128)S(1)}, /*index=5...) while((s32[]{:T(128)}, f32[64,128]{1,0:T(8,128)S(1)}, ...), condition=%wide.region_13.18_spmd, body=%wide.region_10.17_spmd.sunk | while | flops 68558968 | bytes 3252905 | solution.py:32
  369.7 2.8 gather_fusion.14
  376.8 2.8 gather_fusion.14
  383.9 2.8 gather_fusion.14
  391.0 2.8 gather_fusion.14
  402.2 114.2 %pmax.29 = bf16[64,128]{1,0:T(8,128)(2,1)S(1)} all-reduce(bf16[64,128]{1,0:T(8,128)(2,1)S(1)} %convert_element_type.12), channel_id=1, replica_groups=mesh['row'=32,'col'=16] {'row'}, use_global_device_ids=true, to_apply=%region_14.19 | all-reduce | flops 8192 | bytes 32768 | tf_op jit(solution)/shard_map/pmax | solution.py:52
  516.4 45.9 %while.107 = (s32[]{:T(128)}, f32[64,128]{1,0:T(8,128)S(1)}, s32[6,8]{1,0:T(8,128)S(1)}, pred[6,8]{1,0:T(8,128)(4,1)S(1)}, s32[6,8]{1,0:T(8,128)S(1)}, /*index=5...) while((s32[]{:T(128)}, f32[64,128]{1,0:T(8,128)S(1)}, ...), condition=%wide.region_18.23_spmd, body=%wide.region_15.22_spmd.sunk | while | flops 68691064 | bytes 3273425 | solution.py:42
  562.3 90.0 %psum.29 = f32[64,128]{1,0:T(8,128)S(1)} all-reduce(f32[64,128]{1,0:T(8,128)S(1)} %get-tuple-element.1541), channel_id=1, replica_groups=mesh['row'=32,'col'=16] {'row'}, use_global_device_ids=true, to_apply=%region_19.24 | all-reduce | flops 8192 | bytes 65536 | tf_op jit(solution)/shard_map/psum | solution.py:55
  652.3 42.2 %while.108 = (s32[]{:T(128)}, f32[32,128]{1,0:T(8,128)S(1)}, s32[6,8]{1,0:T(8,128)S(1)}, pred[6,8]{1,0:T(8,128)(4,1)S(1)}, s32[6,8]{1,0:T(8,128)S(1)}, /*index=5...) while((s32[]{:T(128)}, f32[32,128]{1,0:T(8,128)S(1)}, ...), condition=%wide.region_23.28_spmd, body=%wide.region_20.27_spmd.sunk | while | flops 68558968 | bytes 3252905 | solution.py:32
  694.6 55.7 %pmax.30 = f32[32,128]{1,0:T(8,128)S(1)} all-reduce(f32[32,128]{1,0:T(8,128)S(1)} %get-tuple-element.1542), channel_id=1, replica_groups=mesh['row'=32,'col'=16] {'col'}, use_global_device_ids=true, to_apply=%region_24.29 | all-reduce | flops 4096 | bytes 32768 | tf_op jit(solution)/shard_map/pmax | solution.py:46
  750.3 45.7 %while.109 = (s32[]{:T(128)}, f32[32,128]{1,0:T(8,128)S(1)}, s32[6,8]{1,0:T(8,128)S(1)}, pred[6,8]{1,0:T(8,128)(4,1)S(1)}, s32[6,8]{1,0:T(8,128)S(1)}, /*index=5...) while((s32[]{:T(128)}, f32[32,128]{1,0:T(8,128)S(1)}, ...), condition=%wide.region_28.33_spmd, body=%wide.region_25.32_spmd.sunk | while | flops 68691064 | bytes 3273425 | solution.py:42
  795.9 56.0 %psum.30 = f32[32,128]{1,0:T(8,128)S(1)} all-reduce(f32[32,128]{1,0:T(8,128)S(1)} %get-tuple-element.1543), channel_id=1, replica_groups=mesh['row'=32,'col'=16] {'col'}, use_global_device_ids=true, to_apply=%region_29.34 | all-reduce | flops 4096 | bytes 32768 | tf_op jit(solution)/shard_map/psum | solution.py:47
  851.9 42.5 %while.110 = (s32[]{:T(128)}, f32[64,128]{1,0:T(8,128)S(1)}, s32[6,8]{1,0:T(8,128)S(1)}, pred[6,8]{1,0:T(8,128)(4,1)S(1)}, s32[6,8]{1,0:T(8,128)S(1)}, /*index=5...) while((s32[]{:T(128)}, f32[64,128]{1,0:T(8,128)S(1)}, ...), condition=%wide.region_33.38_spmd, body=%wide.region_30.37_spmd.sunk | while | flops 68558968 | bytes 3252905 | solution.py:32
  894.5 117.5 %pmax.31 = bf16[64,128]{1,0:T(8,128)(2,1)S(1)} all-reduce(bf16[64,128]{1,0:T(8,128)(2,1)S(1)} %convert_element_type.14), channel_id=1, replica_groups=mesh['row'=32,'col'=16] {'row'}, use_global_device_ids=true, to_apply=%region_34.39 | all-reduce | flops 8192 | bytes 32768 | tf_op jit(solution)/shard_map/pmax | solution.py:52
  1012.0 45.9 %while.111 = (s32[]{:T(128)}, f32[64,128]{1,0:T(8,128)S(1)}, s32[6,8]{1,0:T(8,128)S(1)}, pred[6,8]{1,0:T(8,128)(4,1)S(1)}, s32[6,8]{1,0:T(8,128)S(1)}, /*index=5...) while((s32[]{:T(128)}, f32[64,128]{1,0:T(8,128)S(1)}, ...), condition=%wide.region_38.43_spmd, body=%wide.region_35.42_spmd.sunk | while | flops 68691064 | bytes 3273425 | solution.py:42
  1057.9 90.0 %psum.31 = f32[64,128]{1,0:T(8,128)S(1)} all-reduce(f32[64,128]{1,0:T(8,128)S(1)} %get-tuple-element.1545), channel_id=1, replica_groups=mesh['row'=32,'col'=16] {'row'}, use_global_device_ids=true, to_apply=%region_39.44 | all-reduce | flops 8192 | bytes 65536 | tf_op jit(solution)/shard_map/psum | solution.py:55
  (773 shorter events, 347.0 us)
Async XLA Ops:
  7.2 67.8 %all-gather.4.cloned.1.call-start = ((), (), s32[]{:S(2)}) async-start(), calls=%async_computation | async-start | bytes 2228224 | tf_op jit(solution)/shard_map/all_gather | solution.py:66
  7.9 144.0 %all-gather.6.cloned.1.call-start = ((), (), s32[]{:S(2)}) async-start(), calls=%async_computation.1 | async-start | bytes 4325376 | tf_op jit(solution)/shard_map/all_gather | solution.py:68
  75.0 80.3 %copy-start = (bf16[4096,256]{1,0:T(8,128)(2,1)S(1)}, bf16[4096,256]{1,0:T(8,128)(2,1)}, u32[]{:S(2)}) copy-start(bf16[4096,256]{1,0:T(8,128)(2,1)} %all-gather.4.cloned.1.call-done) | copy-start | bytes 6291460
Sparse Core Ops, SparseCore 0:
  11.0 63.9 all-gather.3
  77.1 74.7 all-gather.5
where the time goes:
time: 1160 us
  blocking collectives  701 us (60%)
  local copies, waits for them, and re-layouts  283 us (24%)
  waiting for transfers between devices  78.4 us (7%)
  other arithmetic  47.9 us (4%)
  matrix products  26.8 us (2%)
  between operations  14.9 us (1%)
    pmax x2, blocking collectives, col_potential(): lax.pmax(local_max(score_of, targets, shape_blocks, turns).astype(jnp.bfl...  232 us
    psum x2, blocking collectives, col_potential(): total = lax.psum(local_sum(score_of, targets, top, turns), 'row')  180 us
    gather x48, local copies, waits for them, and re-layouts, block_costs(): y_take = jnp.take(y_blocks, cols, axis=0)  133 us
    pmax x2, blocking collectives, row_potential(): top = lax.pmax(local_max(score_of, targets, shape_blocks, turns), 'col')  116 us
    psum x2, blocking collectives, row_potential(): total = lax.psum(local_sum(score_of, targets, top, turns), 'col')  112 us
    all_gather x1, waiting for transfers between devices, body(): y_all = lax.all_gather(y_points, 'row', axis=0, tiled=True)  74.6 us
    all_gather x1, blocking collectives, body(): lax.all_gather(jnp.stack([log_b, g_init]), 'row', axis=1, tiled=True)  41.8 us
    gather x48, local copies, waits for them, and re-layouts, block_costs(): x_take = jnp.take(x_blocks, rows, axis=0)  27.8 us
  transfers between devices with their start and end apart: 2, of which 2 were waited for; matrix products, arithmetic and copies ran while one was open for 0% of the time, Pallas kernels for 0%

commit v1 on v0

v1 whole, which is shorter than its diff:
```python
import functools
import math

import jax
import jax.numpy as jnp
from jax import lax
from jax.experimental import pallas as pl
from jax.experimental.pallas import tpu as pltpu
from jax.sharding import PartitionSpec as P

MESH = pl.DeviceIdType.MESH
BLOCK = 128
ITERS = 2
CORES = 2
LOG2E = math.log2(math.e)
LN2 = math.log(2.0)
NEGATIVE = -1e30
TINY = 1e-37
F32 = jnp.float32


def kernel(
    dims,
    tile_ref, count_ref, x_hbm, y_hbm, log_a, log_b, g_init,
    f_out, g_out,
    x_all, y_all, w_all, u_all, kt, kk, tile_top, tile_sum, tile_lse, block_top,
    f_send, f_recv, g_send, g_recv, x_square, y_square,
    in_sem, ring_send, ring_recv, wring_send, wring_recv, mate_sem, xa_send, xa_recv, xb_send, xb_recv,
    f_sem, u_sem, g_sem, w_sem,
):
    nz, nx, ny = dims
    rows, cols = nz * CORES, nx * ny
    tiles = tile_ref.shape[0]
    half = nz // 2
    row, col = lax.axis_index("row"), lax.axis_index("col")
    z, core = row // CORES, row % CORES
    px, py = col // ny, col % ny
    mate = (z * CORES + 1 - core, col)

    def at_z(step):
        return (z + step + nz) % nz * CORES + core

    def at_x(step):
        return (px + step) % nx * ny + py

    def at_y(step):
        return px * ny + (py + step) % ny

    def remote(src, dst, send, recv, device):
        return pltpu.make_async_remote_copy(
            src_ref=src, dst_ref=dst, send_sem=send, recv_sem=recv, device_id=device, device_id_type=MESH
        )

    def drain(ref, sem):
        pltpu.make_async_copy(ref, ref, sem).wait()

    load_x = pltpu.make_async_copy(x_hbm, x_all.at[pl.ds(2 * col, 2)], in_sem.at[0])
    load_y = pltpu.make_async_copy(y_hbm, y_all.at[pl.ds(2 * row, 2)], in_sem.at[1])
    load_y.start()
    load_x.start()

    barrier = pltpu.get_barrier_semaphore()
    greeted = [mate, (at_z(1), col), (at_z(-1), col)]
    greeted += [(row, at_x(k)) for k in range(1, nx)] + [(row, at_y(k)) for k in range(1, ny)]
    for device in greeted:
        pl.semaphore_signal(barrier, inc=1, device_id=device, device_id_type=MESH)
    pl.semaphore_wait(barrier, len(greeted))

    def ring(way, step, part):
        origin = at_z(-(step - 1) if way == 0 else step - 1)
        block = y_all.at[origin * 2 + part]
        return remote(
            block, block, ring_send.at[way, step, part], ring_recv.at[way, step, part],
            (at_z(1 if way == 0 else -1), col),
        )

    def wring(way, step):
        origin = at_z(-(step - 1) if way == 0 else step - 1)
        line = w_all.at[0, origin]
        return remote(
            line, line, wring_send.at[way, step], wring_recv.at[way, step], (at_z(1 if way == 0 else -1), col)
        )

    def to_mate(origin, part):
        block = y_all.at[origin * 2 + part]
        return remote(block, block, mate_sem.at[0], mate_sem.at[1], mate)

    def w_to_mate(origin):
        line = w_all.at[0, origin]
        return remote(line, line, mate_sem.at[2], mate_sem.at[3], mate)

    load_y.wait()
    for part in range(2):
        for way in range(2):
            if half > 1 or part == way:
                ring(way, 1, part).start()
    load_x.wait()
    for k in range(1, nx):
        block = x_all.at[2 * col]
        remote(block, block, xa_send.at[0, k], xa_recv.at[0, k], (row, at_x(k))).start()
    for k in range(1, ny):
        block = x_all.at[2 * col + 1]
        remote(block, block, xa_send.at[1, k], xa_recv.at[1, k], (row, at_y(k))).start()
    for part in range(2):
        to_mate(row, part).start()

    diagonal = lax.broadcasted_iota(jnp.int32, (BLOCK, BLOCK), 0) == lax.broadcasted_iota(
        jnp.int32, (BLOCK, BLOCK), 1
    )

    def squares(block):
        value = block.astype(F32)
        total = jnp.sum(value * value, axis=1, keepdims=True)
        return jnp.sum(jnp.where(diagonal, total, 0.0), axis=0, keepdims=True)

    for part in range(2):
        y_square[part : part + 1, :] = squares(y_all[2 * row + part])
    w_all[0, row] = LOG2E * (4.0 * g_init[...] - 2.0 * y_square[...] + log_b[...])
    wring(0, 1).start()
    if half > 1:
        wring(1, 1).start()
    w_to_mate(row).start()
    for part in range(2):
        x_square[part : part + 1, :] = squares(x_all[2 * col + part])

    def send_plane():
        for k in range(nx):
            if k:
                block = x_all.at[2 * at_x(nx - k)]
                remote(block, block, xa_send.at[0, k], xa_recv.at[0, k], (row, col)).wait_recv()
            block = x_all.at[2 * at_x(nx - k)]
            for j in range(1, ny):
                remote(block, block, xb_send.at[0], xb_recv.at[0], (row, at_y(j))).start()
        for k in range(ny):
            if k:
                block = x_all.at[2 * at_y(ny - k) + 1]
                remote(block, block, xa_send.at[1, k], xa_recv.at[1, k], (row, col)).wait_recv()
            block = x_all.at[2 * at_y(ny - k) + 1]
            for j in range(1, nx):
                remote(block, block, xb_send.at[1], xb_recv.at[1], (row, at_x(j))).start()

    for step in range(1, half + 1):
        last, before_last = step == half, step == half - 1
        for part in range(2):
            for way in range(2):
                if last and part != way:
                    continue
                origin = at_z(-step if way == 0 else step)
                ring(way, step, part).wait_recv()
                if not last and not (before_last and part != way):
                    ring(way, step + 1, part).start()
                to_mate(origin, part).start()
                if part == 1 and not last:
                    wring(way, step).wait_recv()
                    if not (before_last and way == 1):
                        wring(way, step + 1).start()
                    w_to_mate(origin).start()
        if last:
            wring(0, step).wait_recv()
            w_to_mate(at_z(-step)).start()
        if step == min(2, half):
            send_plane()

    for lane, (outer, inner) in enumerate(((nx, ny), (ny, nx))):
        if inner > 1:
            drain(x_all.at[pl.ds(0, outer * (inner - 1))], xb_recv.at[lane])
    drain(y_all.at[pl.ds(0, rows)], mate_sem.at[1])
    drain(w_all.at[0, pl.ds(0, nz)], mate_sem.at[3])

    def row_id(t):
        return tile_ref[t, 0] % (2 * cols)

    def col_id(t):
        block = tile_ref[t, 1]
        return block // (2 * cols) * 2 + block % 2

    def column_of(line):
        return jnp.transpose(jnp.broadcast_to(line, (BLOCK, BLOCK)))

    def reduce_tile(t, scores):
        top = jnp.max(scores, axis=0, keepdims=True)
        tile_top[pl.ds(t, 1), :] = top
        tile_sum[pl.ds(t, 1), :] = jnp.sum(jnp.exp2(scores - top), axis=0, keepdims=True)

    def product(left, right):
        return lax.dot_general(left, right, (((1,), (1,)), ((), ())), preferred_element_type=F32) * (4.0 * LOG2E)

    def loop(body, unroll):
        def step(t, carry):
            body(t)
            return carry

        lax.fori_loop(0, tiles, step, 0, unroll=unroll)

    def combine(id_of, blocks):
        alive = lax.broadcasted_iota(jnp.int32, (tiles, BLOCK), 0) < count_ref[0]
        tile_lse[...] = jnp.where(alive, tile_top[...] + jnp.log2(tile_sum[...]), NEGATIVE)
        place = lax.broadcasted_iota(jnp.int32, (blocks, BLOCK), 0)

        def top_of(t, top):
            return jnp.maximum(top, jnp.where(place == id_of(t), tile_lse[pl.ds(t, 1), :], NEGATIVE))

        top = lax.fori_loop(0, tiles, top_of, jnp.full((blocks, BLOCK), NEGATIVE, F32), unroll=4)
        block_top[pl.ds(0, blocks), :] = top

        def sum_of(t, total):
            home = id_of(t)
            share = jnp.exp2(tile_lse[pl.ds(t, 1), :] - block_top[pl.ds(home, 1), :])
            return total + jnp.where(place == home, share, 0.0)

        total = lax.fori_loop(0, tiles, sum_of, jnp.zeros((blocks, BLOCK), F32), unroll=4)
        return top + jnp.log2(jnp.maximum(total, TINY))

    def merge(parts):
        top = jnp.max(parts, axis=0)
        return top + jnp.log2(jnp.sum(jnp.exp2(parts - top[None]), axis=0))

    def spread(value, out):
        for k in range(value.shape[0] // 2):
            out[k] = value[2 * k : 2 * k + 2, :]

    def each(count, body):
        def step(k, carry):
            body(k)
            return carry

        lax.fori_loop(1, count, step, 0)

    for it in range(ITERS):
        def f_tile(t):
            line, part = col_id(t) // 2, col_id(t) % 2
            if it == 0:
                kt[t] = product(y_all[col_id(t)], x_all[row_id(t)])
            reduce_tile(t, kt[t] + column_of(w_all[it, line, pl.ds(part, 1), :]))

        loop(f_tile, 2)
        spread(combine(row_id, cols * 2), f_send.at[it])

        def send_f(k):
            owner = (col + k) % cols
            remote(
                f_send.at[it, owner], f_recv.at[it, col], f_sem.at[it, 0], f_sem.at[it, 1], (row, owner)
            ).start()

        each(cols, send_f)
        f_recv[it, col] = f_send[it, col]
        if it == 0:

            def other(t):
                kk[t] = product(x_all[row_id(t)], y_all[col_id(t)])

            loop(other, 2)
        drain(f_recv.at[it, pl.ds(0, cols - 1)], f_sem.at[it, 1])
        lse = merge(f_recv[it])
        u_all[it, col] = LOG2E * log_a[...] - lse

        def send_u(k):
            line = u_all.at[it, col]
            remote(line, line, u_sem.at[it, 0], u_sem.at[it, 1], (row, (col + k) % cols)).start()

        each(cols, send_u)
        if it == ITERS - 1:
            f_out[...] = 0.5 * x_square[...] - (0.25 * LN2) * lse
        drain(u_all.at[it, pl.ds(0, cols - 1)], u_sem.at[it, 1])

        def g_tile(t):
            line, part = row_id(t) // 2, row_id(t) % 2
            reduce_tile(t, kk[t] + column_of(u_all[it, line, pl.ds(part, 1), :]))

        loop(g_tile, 2)
        spread(combine(col_id, rows * 2), g_send.at[it])

        def send_g(k):
            owner = (row + k) % rows
            remote(
                g_send.at[it, owner], g_recv.at[it, row], g_sem.at[it, 0], g_sem.at[it, 1], (owner, col)
            ).start()

        each(rows, send_g)
        g_recv[it, row] = g_send[it, row]
        drain(g_recv.at[it, pl.ds(0, rows - 1)], g_sem.at[it, 1])
        lse = merge(g_recv[it])
        if it == ITERS - 1:
            g_out[...] = 0.5 * y_square[...] - (0.25 * LN2) * lse
        else:
            w_all[it + 1, row] = LOG2E * log_b[...] - lse

            def send_w(k):
                line = w_all.at[it + 1, row]
                remote(line, line, w_sem.at[it, 0], w_sem.at[it, 1], ((row + k) % rows, col)).start()

            each(rows, send_w)
            drain(w_all.at[it + 1, pl.ds(0, rows - 1)], w_sem.at[it, 1])

    for part in range(2):
        for way in range(2):
            for step in range(1, half + 1):
                if not (step == half and part != way):
                    ring(way, step, part).wait_send()
    for step in range(1, half + 1):
        wring(0, step).wait_send()
        if step < half:
            wring(1, step).wait_send()
    drain(y_all.at[pl.ds(0, rows)], mate_sem.at[0])
    drain(w_all.at[0, pl.ds(0, nz)], mate_sem.at[2])
    for lane, (outer, inner) in enumerate(((nx, ny), (ny, nx))):
        for k in range(1, outer):
            block = x_all.at[0]
            remote(block, block, xa_send.at[lane, k], xa_recv.at[lane, k], (row, at_x(1))).wait_send()
        if inner > 1:
            drain(x_all.at[pl.ds(0, outer * (inner - 1))], xb_send.at[lane])
    for it in range(ITERS):
        drain(f_recv.at[it, pl.ds(0, cols - 1)], f_sem.at[it, 0])
        drain(u_all.at[it, pl.ds(0, cols - 1)], u_sem.at[it, 0])
        drain(g_recv.at[it, pl.ds(0, rows - 1)], g_sem.at[it, 0])
        if it < ITERS - 1:
            drain(w_all.at[it + 1, pl.ds(0, rows - 1)], w_sem.at[it, 0])


def body(dims, x_points, y_points, log_a, log_b, g_init, tile_list, tile_count):
    nz, nx, ny = dims
    rows, cols = nz * CORES, nx * ny
    width = x_points.shape[1]
    tiles = tile_list.shape[0]
    half = nz // 2
    vmem = pl.BlockSpec(memory_space=pltpu.VMEM)
    smem = pl.BlockSpec(memory_space=pltpu.SMEM)
    anywhere = pl.BlockSpec(memory_space=pl.ANY)
    dma = pltpu.SemaphoreType.DMA
    line = jax.ShapeDtypeStruct((2, BLOCK), F32)
    f_out, g_out = pl.pallas_call(
        functools.partial(kernel, dims),
        out_shape=(line, line),
        in_specs=[smem, smem, anywhere, anywhere, vmem, vmem, vmem],
        out_specs=(vmem, vmem),
        scratch_shapes=[
            pltpu.VMEM((cols * 2, BLOCK, width), jnp.bfloat16),
            pltpu.VMEM((rows * 2, BLOCK, width), jnp.bfloat16),
            pltpu.VMEM((ITERS, rows, 2, BLOCK), F32),
            pltpu.VMEM((ITERS, cols, 2, BLOCK), F32),
            pltpu.VMEM((tiles, BLOCK, BLOCK), F32),
            pltpu.VMEM((tiles, BLOCK, BLOCK), F32),
            pltpu.VMEM((tiles, BLOCK), F32),
            pltpu.VMEM((tiles, BLOCK), F32),
            pltpu.VMEM((tiles, BLOCK), F32),
            pltpu.VMEM((max(rows, cols) * 2, BLOCK), F32),
            pltpu.VMEM((ITERS, cols, 2, BLOCK), F32),
            pltpu.VMEM((ITERS, cols, 2, BLOCK), F32),
            pltpu.VMEM((ITERS, rows, 2, BLOCK), F32),
            pltpu.VMEM((ITERS, rows, 2, BLOCK), F32),
            pltpu.VMEM((2, BLOCK), F32),
            pltpu.VMEM((2, BLOCK), F32),
            dma((2,)),
            dma((2, half + 1, 2)),
            dma((2, half + 1, 2)),
            dma((2, half + 1)),
            dma((2, half + 1)),
            dma((4,)),
            dma((2, max(nx, ny))),
            dma((2, max(nx, ny))),
            dma((2,)),
            dma((2,)),
            dma((ITERS, 2)),
            dma((ITERS, 2)),
            dma((ITERS, 2)),
            dma((ITERS, 2)),
        ],
        compiler_params=pltpu.CompilerParams(collective_id=0, has_side_effects=True),
    )(
        tile_list,
        tile_count,
        x_points.reshape(2, BLOCK, width),
        y_points.reshape(2, BLOCK, width),
        log_a.reshape(2, BLOCK),
        log_b.reshape(2, BLOCK),
        g_init.reshape(2, BLOCK),
    )
    return f_out.reshape(-1), g_out.reshape(-1)


def solution(mesh):
    rows, cols = mesh.shape["row"], mesh.shape["col"]
    side = math.isqrt(cols)
    dims = (rows // CORES, cols // side, side)
    whole = P(("row", "col"))
    grid = P(("row", "col"), None)
    return jax.shard_map(
        functools.partial(body, dims),
        mesh=mesh,
        in_specs=(grid, grid, whole, whole, whole, grid, whole),
        out_specs=(whole, whole),
        check_vma=False,
    )
```

time: 1160 us -> 115 us (0.10)
  blocking collectives: 701 us -> 0 us
  local copies, waits for them, and re-layouts: 283 us -> 3.26 us
  Pallas kernels: 0 us -> 110 us
  waiting for transfers between devices: 78.4 us -> 0 us
  other arithmetic: 47.9 us -> 0 us
  matrix products: 26.8 us -> 0 us
  between operations: 14.9 us -> 1.3 us
    pmax x4 -> x0, blocking collectives: 348 us -> none  [the longest x2 232 us: col_potential(): lax.pmax(local_max(score_of, targets, shape_blocks, turns).astype(jnp.bfl...]
    psum x4 -> x0, blocking collectives: 292 us -> none  [the longest x2 180 us: col_potential(): total = lax.psum(local_sum(score_of, targets, top, turns), 'row')]
    gather x312 -> x0, local copies, waits for them, and re-layouts: 281 us -> none  [the longest x48 133 us: block_costs(): y_take = jnp.take(y_blocks, cols, axis=0)]
    pallas_call x0 -> x1, Pallas kernels: none -> 110 us  [body(): pl.pallas_call(functools.partial(kernel, dims), out_shape=(line, line), i...]
    all_gather x2 -> x0, waiting for transfers between devices: 77.1 us -> none  [the longest x1 74.6 us: body(): y_all = lax.all_gather(y_points, 'row', axis=0, tiled=True)]
    all_gather x2 -> x0, blocking collectives: 61.4 us -> none  [the longest x1 41.8 us: body(): lax.all_gather(jnp.stack([log_b, g_init]), 'row', axis=1, tiled=True)]
    dot_general x48 -> x0, matrix products: 26.8 us -> none  [block_costs(): jnp.einsum('tpd,tqd->tpq', x_take, y_take, preferred_element_type=jnp.flo...]
    another operation x25 -> x0, other arithmetic: 16.6 us -> none  [the longest x24 15.9 us: visit(): acc.at[targets[turn_index]].max(jnp.max(score_of(turn_index), axis=-1))]
  transfers between devices with their start and end apart: 2 -> 0, of which waited for: 2 -> 0; matrix products, arithmetic and copies ran while one was open for 0% -> 0% of each run, Pallas kernels for 0% -> 0%
where the time goes in v1:
time: 115 us
  Pallas kernels  110 us (96%)
  local copies, waits for them, and re-layouts  3.26 us (3%)
  between operations  1.3 us (1%)
    pallas_call x1, Pallas kernels, body(): pl.pallas_call(functools.partial(kernel, dims), out_shape=(line, line), i...  110 us
    unnamed x9, local copies, waits for them, and re-layouts  3.26 us

profile of v1, /device:TPU:1, one launch (start us, length us, event | category | flops | bytes accessed | tf_op | source)
XLA Modules:
  0.0 114.9 jit_solution(7734374270298197162)
XLA Ops:
  1.3 0.0 copy-start
  1.3 0.7 copy-done
  2.0 0.7 copy.9.tile_ref
  2.6 110.3 %shard_map.86 = (f32[2,128]{1,0:T(2,128)}, f32[2,128]{1,0:T(2,128)}) custom-call(s32[48,2]{1,0:T(8,128)} %copy.9.tile_ref, s32[1]{0:T(128)S(6)} %copy.12.count_ref, bf16[2,128,256]{2,1,0:T(8,128)(2,1)} %bitcast.7, bf16[2,128,256]{2,1,0:T(8,128)(2,1)} %bitcast.8, f32[2,128]{1,0:T(2,128)} %bitcast.9, f32[2,128]{1,0:T(2,128)} %bitcast.10, f32[2,128]{1,0:T(2,128)} %bitcast.11), custom_call_target="tpu_custom_call" | custom-call | tf_op jit(solution)/shard_map/pallas_call | solution.py:331
  113.0 0.0 copy-start.2
  113.0 0.7 copy-done.2
  113.6 0.0 copy-start.1
  113.6 0.6 copy.13
  114.2 0.1 copy-done.1
  114.3 0.6 copy.14
Async XLA Ops:
  1.3 0.7 copy-start
  113.0 0.7 copy-start.2
  113.6 0.7 copy-start.1

commit v2 on v1

--- a/solution.py
+++ b/solution.py
@@ -17,6 +17,8 @@
 NEGATIVE = -1e30
 TINY = 1e-37
 F32 = jnp.float32
+PIECES = 4
+UNROLL = 8
 
 
 def kernel(
@@ -25,12 +27,12 @@
     f_out, g_out,
     x_all, y_all, w_all, u_all, kt, kk, tile_top, tile_sum, tile_lse, block_top,
     f_send, f_recv, g_send, g_recv, x_square, y_square,
-    in_sem, ring_send, ring_recv, wring_send, wring_recv, mate_sem, xa_send, xa_recv, xb_send, xb_recv,
+    in_sem, ring_send, ring_recv, wring_send, wring_recv, mate_sem, xa_send, xa_recv,
     f_sem, u_sem, g_sem, w_sem,
 ):
     nz, nx, ny = dims
     rows, cols = nz * CORES, nx * ny
-    tiles = tile_ref.shape[0]
+    tiles = tile_ref.shape[1]
     half = nz // 2
     row, col = lax.axis_index("row"), lax.axis_index("col")
     z, core = row // CORES, row % CORES
@@ -54,6 +56,11 @@
     def drain(ref, sem):
         pltpu.make_async_copy(ref, ref, sem).wait()
 
+    pending = []
+
+    def later(wait, *args):
+        pending.append(lambda: wait(*args))
+
     load_x = pltpu.make_async_copy(x_hbm, x_all.at[pl.ds(2 * col, 2)], in_sem.at[0])
     load_y = pltpu.make_async_copy(y_hbm, y_all.at[pl.ds(2 * row, 2)], in_sem.at[1])
     load_y.start()
@@ -61,14 +68,19 @@
 
     barrier = pltpu.get_barrier_semaphore()
     greeted = [mate, (at_z(1), col), (at_z(-1), col)]
-    greeted += [(row, at_x(k)) for k in range(1, nx)] + [(row, at_y(k)) for k in range(1, ny)]
+    greeted += [(row, at_x(1)), (row, at_x(nx - 1)), (row, at_y(1)), (row, at_y(ny - 1))]
     for device in greeted:
         pl.semaphore_signal(barrier, inc=1, device_id=device, device_id_type=MESH)
     pl.semaphore_wait(barrier, len(greeted))
 
+
+    size = 2 * BLOCK // PIECES
+
+    def piece(origin, part):
+        return y_all.at[origin * 2 + part * size // BLOCK, pl.ds(part * size % BLOCK, size)]
+
     def ring(way, step, part):
-        origin = at_z(-(step - 1) if way == 0 else step - 1)
-        block = y_all.at[origin * 2 + part]
+        block = piece(at_z(-(step - 1) if way == 0 else step - 1), part)
         return remote(
             block, block, ring_send.at[way, step, part], ring_recv.at[way, step, part],
             (at_z(1 if way == 0 else -1), col),
@@ -82,26 +94,51 @@
         )
 
     def to_mate(origin, part):
-        block = y_all.at[origin * 2 + part]
+        block = piece(origin, part)
         return remote(block, block, mate_sem.at[0], mate_sem.at[1], mate)
 
     def w_to_mate(origin):
         line = w_all.at[0, origin]
         return remote(line, line, mate_sem.at[2], mate_sem.at[3], mate)
 
+    def go(copy):
+        copy.start()
+        later(copy.wait_send)
+
+    def travels(way, step, part):
+        return 1 <= step < half or (step == half and (part < PIECES // 2) == (way == 0))
+
+    def at_line(axis, step):
+        return at_x(step) if axis == 0 else at_y(step)
+
+    def at_both(axis, one, two):
+        x, y = (one, two) if axis == 0 else (two, one)
+        return (px + x + nx) % nx * ny + (py + y + ny) % ny
+
+    def plane(lane, phase, way, hop, index):
+        axis = lane if phase == 0 else 1 - lane
+        sign = 1 if way == 0 else -1
+        back = 0 if hop == 0 else -sign
+        origin = at_both(lane, back, 0) if phase == 0 else at_both(lane, index, back)
+        block = x_all.at[2 * origin + lane]
+        if hop == 1:
+            block = block.at[pl.ds(way * (BLOCK // 2), BLOCK // 2)]
+        sems = (lane, phase, way, hop, index)
+        return remote(block, block, xa_send.at[sems], xa_recv.at[sems], (row, at_line(axis, sign)))
+
     load_y.wait()
-    for part in range(2):
+    for part in range(PIECES):
         for way in range(2):
-            if half > 1 or part == way:
-                ring(way, 1, part).start()
+            if travels(way, 1, part):
+                go(ring(way, 1, part))
     load_x.wait()
-    for k in range(1, nx):
-        block = x_all.at[2 * col]
-        remote(block, block, xa_send.at[0, k], xa_recv.at[0, k], (row, at_x(k))).start()
-    for k in range(1, ny):
-        block = x_all.at[2 * col + 1]
-        remote(block, block, xa_send.at[1, k], xa_recv.at[1, k], (row, at_y(k))).start()
-    for part in range(2):
+    for lane in range(2):
+        for way in range(2):
+            go(plane(lane, 0, way, 0, 0))
+    for lane in range(2):
+        for way in range(2):
+            go(plane(lane, 1, way, 0, 0))
+    for part in range(PIECES):
         to_mate(row, part).start()
 
     diagonal = lax.broadcasted_iota(jnp.int32, (BLOCK, BLOCK), 0) == lax.broadcasted_iota(
@@ -116,66 +153,70 @@
     for part in range(2):
         y_square[part : part + 1, :] = squares(y_all[2 * row + part])
     w_all[0, row] = LOG2E * (4.0 * g_init[...] - 2.0 * y_square[...] + log_b[...])
-    wring(0, 1).start()
-    if half > 1:
-        wring(1, 1).start()
+    go(wring(0, 1))
+    go(wring(1, 1))
     w_to_mate(row).start()
     for part in range(2):
         x_square[part : part + 1, :] = squares(x_all[2 * col + part])
 
-    def send_plane():
-        for k in range(nx):
-            if k:
-                block = x_all.at[2 * at_x(nx - k)]
-                remote(block, block, xa_send.at[0, k], xa_recv.at[0, k], (row, col)).wait_recv()
-            block = x_all.at[2 * at_x(nx - k)]
-            for j in range(1, ny):
-                remote(block, block, xb_send.at[0], xb_recv.at[0], (row, at_y(j))).start()
-        for k in range(ny):
-            if k:
-                block = x_all.at[2 * at_y(ny - k) + 1]
-                remote(block, block, xa_send.at[1, k], xa_recv.at[1, k], (row, col)).wait_recv()
-            block = x_all.at[2 * at_y(ny - k) + 1]
-            for j in range(1, nx):
-                remote(block, block, xb_send.at[1], xb_recv.at[1], (row, at_x(j))).start()
-
-    for step in range(1, half + 1):
-        last, before_last = step == half, step == half - 1
-        for part in range(2):
+    def plane_steps(stage):
+        for lane in range(2):
+            if stage == 1:
+                for way in range(2):
+                    plane(lane, 0, way, 0, 0).wait_recv()
+                    go(plane(lane, 0, way, 1, 0))
+                    for out in range(2):
+                        go(plane(lane, 1, out, 0, 3 if way == 0 else 1))
+            if stage == 2:
+                for way in range(2):
+                    plane(lane, 0, way, 1, 0).wait_recv()
+                for out in range(2):
+                    go(plane(lane, 1, out, 0, 2))
+            if stage in (1, 2, 3, 4):
+                index = (0, 0, 1, 3, 2)[stage]
+                for way in range(2):
+                    plane(lane, 1, way, 0, index).wait_recv()
+                    go(plane(lane, 1, way, 1, index))
+            if stage == 5:
+                for index in range(4):
+                    for way in range(2):
+                        plane(lane, 1, way, 1, index).wait_recv()
+
+    def pass_lines(step):
+        for way in range(2):
+            if 1 <= step < half or (step == half and way == 0):
+                wring(way, step).wait_recv()
+                if step + 1 < half or (step + 1 == half and way == 0):
+                    go(wring(way, step + 1))
+                w_to_mate(at_z(-step if way == 0 else step)).start()
+
+    for step in range(1, max(half, 5) + 1):
+        for part in range(PIECES):
             for way in range(2):
-                if last and part != way:
+                if not travels(way, step, part):
                     continue
-                origin = at_z(-step if way == 0 else step)
                 ring(way, step, part).wait_recv()
-                if not last and not (before_last and part != way):
-                    ring(way, step + 1, part).start()
-                to_mate(origin, part).start()
-                if part == 1 and not last:
-                    wring(way, step).wait_recv()
-                    if not (before_last and way == 1):
-                        wring(way, step + 1).start()
-                    w_to_mate(origin).start()
-        if last:
-            wring(0, step).wait_recv()
-            w_to_mate(at_z(-step)).start()
-        if step == min(2, half):
-            send_plane()
-
-    for lane, (outer, inner) in enumerate(((nx, ny), (ny, nx))):
-        if inner > 1:
-            drain(x_all.at[pl.ds(0, outer * (inner - 1))], xb_recv.at[lane])
+                if travels(way, step + 1, part):
+                    go(ring(way, step + 1, part))
+                to_mate(at_z(-step if way == 0 else step), part).start()
+            if part == 0 and step <= half:
+                pass_lines(step - 1)
+        plane_steps(step)
+    pass_lines(half)
     drain(y_all.at[pl.ds(0, rows)], mate_sem.at[1])
+    later(drain, y_all.at[pl.ds(0, rows)], mate_sem.at[0])
     drain(w_all.at[0, pl.ds(0, nz)], mate_sem.at[3])
+    later(drain, w_all.at[0, pl.ds(0, nz)], mate_sem.at[2])
 
     def row_id(t):
-        return tile_ref[t, 0] % (2 * cols)
+        return tile_ref[0, t] % (2 * cols)
 
     def col_id(t):
-        block = tile_ref[t, 1]
+        block = tile_ref[1, t]
         return block // (2 * cols) * 2 + block % 2
 
     def column_of(line):
-        return jnp.transpose(jnp.broadcast_to(line, (BLOCK, BLOCK)))
+        return jnp.sum(jnp.where(diagonal, line, 0.0), axis=1, keepdims=True)
 
     def reduce_tile(t, scores):
         top = jnp.max(scores, axis=0, keepdims=True)
@@ -221,7 +262,7 @@
 
     def each(count, body):
         def step(k, carry):
-            body(k)
+            body(count // 2 + k // 2 * (1 - k % 2 * 2))
             return carry
 
         lax.fori_loop(1, count, step, 0)
@@ -233,7 +274,7 @@
                 kt[t] = product(y_all[col_id(t)], x_all[row_id(t)])
             reduce_tile(t, kt[t] + column_of(w_all[it, line, pl.ds(part, 1), :]))
 
-        loop(f_tile, 2)
+        loop(f_tile, UNROLL)
         spread(combine(row_id, cols * 2), f_send.at[it])
 
         def send_f(k):
@@ -243,13 +284,14 @@
             ).start()
 
         each(cols, send_f)
+        later(drain, f_recv.at[it, pl.ds(0, cols - 1)], f_sem.at[it, 0])
         f_recv[it, col] = f_send[it, col]
         if it == 0:
 
             def other(t):
                 kk[t] = product(x_all[row_id(t)], y_all[col_id(t)])
 
-            loop(other, 2)
+            loop(other, 4)
         drain(f_recv.at[it, pl.ds(0, cols - 1)], f_sem.at[it, 1])
         lse = merge(f_recv[it])
         u_all[it, col] = LOG2E * log_a[...] - lse
@@ -259,6 +301,7 @@
             remote(line, line, u_sem.at[it, 0], u_sem.at[it, 1], (row, (col + k) % cols)).start()
 
         each(cols, send_u)
+        later(drain, u_all.at[it, pl.ds(0, cols - 1)], u_sem.at[it, 0])
         if it == ITERS - 1:
             f_out[...] = 0.5 * x_square[...] - (0.25 * LN2) * lse
         drain(u_all.at[it, pl.ds(0, cols - 1)], u_sem.at[it, 1])
@@ -267,7 +310,7 @@
             line, part = row_id(t) // 2, row_id(t) % 2
             reduce_tile(t, kk[t] + column_of(u_all[it, line, pl.ds(part, 1), :]))
 
-        loop(g_tile, 2)
+        loop(g_tile, UNROLL)
         spread(combine(col_id, rows * 2), g_send.at[it])
 
         def send_g(k):
@@ -277,6 +320,7 @@
             ).start()
 
         each(rows, send_g)
+        later(drain, g_recv.at[it, pl.ds(0, rows - 1)], g_sem.at[it, 0])
         g_recv[it, row] = g_send[it, row]
         drain(g_recv.at[it, pl.ds(0, rows - 1)], g_sem.at[it, 1])
         lse = merge(g_recv[it])
@@ -290,31 +334,11 @@
                 remote(line, line, w_sem.at[it, 0], w_sem.at[it, 1], ((row + k) % rows, col)).start()
 
             each(rows, send_w)
+            later(drain, w_all.at[it + 1, pl.ds(0, rows - 1)], w_sem.at[it, 0])
             drain(w_all.at[it + 1, pl.ds(0, rows - 1)], w_sem.at[it, 1])
 
-    for part in range(2):
-        for way in range(2):
-            for step in range(1, half + 1):
-                if not (step == half and part != way):
-                    ring(way, step, part).wait_send()
-    for step in range(1, half + 1):
-        wring(0, step).wait_send()
-        if step < half:
-            wring(1, step).wait_send()
-    drain(y_all.at[pl.ds(0, rows)], mate_sem.at[0])
-    drain(w_all.at[0, pl.ds(0, nz)], mate_sem.at[2])
-    for lane, (outer, inner) in enumerate(((nx, ny), (ny, nx))):
-        for k in range(1, outer):
-            block = x_all.at[0]
-            remote(block, block, xa_send.at[lane, k], xa_recv.at[lane, k], (row, at_x(1))).wait_send()
-        if inner > 1:
-            drain(x_all.at[pl.ds(0, outer * (inner - 1))], xb_send.at[lane])
-    for it in range(ITERS):
-        drain(f_recv.at[it, pl.ds(0, cols - 1)], f_sem.at[it, 0])
-        drain(u_all.at[it, pl.ds(0, cols - 1)], u_sem.at[it, 0])
-        drain(g_recv.at[it, pl.ds(0, rows - 1)], g_sem.at[it, 0])
-        if it < ITERS - 1:
-            drain(w_all.at[it + 1, pl.ds(0, rows - 1)], w_sem.at[it, 0])
+    for wait in pending:
+        wait()
 
 
 def body(dims, x_points, y_points, log_a, log_b, g_init, tile_list, tile_count):
@@ -351,15 +375,13 @@
             pltpu.VMEM((2, BLOCK), F32),
             pltpu.VMEM((2, BLOCK), F32),
             dma((2,)),
-            dma((2, half + 1, 2)),
-            dma((2, half + 1, 2)),
+            dma((2, half + 1, PIECES)),
+            dma((2, half + 1, PIECES)),
             dma((2, half + 1)),
             dma((2, half + 1)),
             dma((4,)),
-            dma((2, max(nx, ny))),
-            dma((2, max(nx, ny))),
-            dma((2,)),
-            dma((2,)),
+            dma((2, 2, 2, 2, 4)),
+            dma((2, 2, 2, 2, 4)),
             dma((ITERS, 2)),
             dma((ITERS, 2)),
             dma((ITERS, 2)),
@@ -367,7 +389,7 @@
         ],
         compiler_params=pltpu.CompilerParams(collective_id=0, has_side_effects=True),
     )(
-        tile_list,
+        tile_list.T,
         tile_count,
         x_points.reshape(2, BLOCK, width),
         y_points.reshape(2, BLOCK, width),

time: 115 us -> 103 us (0.90)
  Pallas kernels: 110 us -> 100 us
  local copies, waits for them, and re-layouts: 3.26 us -> 1.86 us
    pallas_call x1, Pallas kernels: 110 us -> 100 us  [body(): pl.pallas_call(functools.partial(kernel, dims), out_shape=(line, line), i...]
    unnamed x9 -> x6, local copies, waits for them, and re-layouts: 3.26 us -> 1.86 us
where the time goes in v2:
time: 103 us
  Pallas kernels  100 us (97%)
  local copies, waits for them, and re-layouts  1.86 us (2%)
  between operations  1.3 us (1%)
    pallas_call x1, Pallas kernels, body(): pl.pallas_call(functools.partial(kernel, dims), out_shape=(line, line), i...  100 us

profile of v2, /device:TPU:1, one launch (start us, length us, event | category | flops | bytes accessed | tf_op | source)
XLA Modules:
  0.0 103.3 jit_solution(8435113625597694611)
XLA Ops:
  1.3 100.2 %shard_map.86 = (f32[2,128]{1,0:T(2,128)}, f32[2,128]{1,0:T(2,128)}) custom-call(s32[2,48]{1,0:T(2,128)} %bitcast.10, s32[1]{0:T(128)S(6)} %copy.11.count_ref, bf16[2,128,256]{2,1,0:T(8,128)(2,1)} %bitcast.8, bf16[2,128,256]{2,1,0:T(8,128)(2,1)} %bitcast.9, f32[2,128]{1,0:T(2,128)} %bitcast.11, f32[2,128]{1,0:T(2,128)} %bitcast.12, f32[2,128]{1,0:T(2,128)} %bitcast.13), custom_call_target="tpu_custom_call" | custom-call | tf_op jit(solution)/shard_map/pallas_call | solution.py:355
  101.4 0.0 copy-start.1
  101.4 0.7 copy-done.1
  102.1 0.0 copy-start
  102.1 0.6 copy.12
  102.7 0.1 copy-done
  102.7 0.6 copy.13
Async XLA Ops:
  101.4 0.7 copy-start.1
  102.1 0.6 copy-start

commit v3 on v2

--- a/solution.py
+++ b/solution.py
@@ -25,7 +25,7 @@
     dims,
     tile_ref, count_ref, x_hbm, y_hbm, log_a, log_b, g_init,
     f_out, g_out,
-    x_all, y_all, w_all, u_all, kt, kk, tile_top, tile_sum, tile_lse, block_top,
+    x_all, y_all, w_all, u_all, a_all, a_rows, kt, kk, tile_top, tile_sum, tile_lse, block_top,
     f_send, f_recv, g_send, g_recv, x_square, y_square,
     in_sem, ring_send, ring_recv, wring_send, wring_recv, mate_sem, xa_send, xa_recv,
     f_sem, u_sem, g_sem, w_sem,
@@ -154,7 +154,8 @@
         y_square[part : part + 1, :] = squares(y_all[2 * row + part])
     w_all[0, row] = LOG2E * (4.0 * g_init[...] - 2.0 * y_square[...] + log_b[...])
     go(wring(0, 1))
-    go(wring(1, 1))
+    if half > 1:
+        go(wring(1, 1))
     w_to_mate(row).start()
     for part in range(2):
         x_square[part : part + 1, :] = squares(x_all[2 * col + part])
@@ -267,6 +268,14 @@
 
         lax.fori_loop(1, count, step, 0)
 
+    a_all[col] = log_a[...]
+
+    def send_a(k):
+        remote(log_a, a_all.at[col], u_sem.at[0, 0], u_sem.at[0, 1], (row, (col + k) % cols)).start()
+
+    each(cols, send_a)
+    later(drain, a_all.at[pl.ds(0, cols - 1)], u_sem.at[0, 0])
+
     for it in range(ITERS):
         def f_tile(t):
             line, part = col_id(t) // 2, col_id(t) % 2
@@ -275,40 +284,36 @@
             reduce_tile(t, kt[t] + column_of(w_all[it, line, pl.ds(part, 1), :]))
 
         loop(f_tile, UNROLL)
-        spread(combine(row_id, cols * 2), f_send.at[it])
+        f_send[it] = combine(row_id, cols * 2)
 
         def send_f(k):
-            owner = (col + k) % cols
             remote(
-                f_send.at[it, owner], f_recv.at[it, col], f_sem.at[it, 0], f_sem.at[it, 1], (row, owner)
+                f_send.at[it], f_recv.at[it, col], f_sem.at[it, 0], f_sem.at[it, 1], (row, (col + k) % cols)
             ).start()
 
         each(cols, send_f)
         later(drain, f_recv.at[it, pl.ds(0, cols - 1)], f_sem.at[it, 0])
-        f_recv[it, col] = f_send[it, col]
+        f_recv[it, col] = f_send[it]
         if it == 0:
 
             def other(t):
                 kk[t] = product(x_all[row_id(t)], y_all[col_id(t)])
 
             loop(other, 4)
+            drain(a_all.at[pl.ds(0, cols - 1)], u_sem.at[0, 1])
+            for k in range(cols):
+                a_rows[2 * k : 2 * k + 2, :] = a_all[k]
         drain(f_recv.at[it, pl.ds(0, cols - 1)], f_sem.at[it, 1])
         lse = merge(f_recv[it])
-        u_all[it, col] = LOG2E * log_a[...] - lse
-
-        def send_u(k):
-            line = u_all.at[it, col]
-            remote(line, line, u_sem.at[it, 0], u_sem.at[it, 1], (row, (col + k) % cols)).start()
-
-        each(cols, send_u)
-        later(drain, u_all.at[it, pl.ds(0, cols - 1)], u_sem.at[it, 0])
+        u_all[...] = LOG2E * a_rows[...] - lse
         if it == ITERS - 1:
-            f_out[...] = 0.5 * x_square[...] - (0.25 * LN2) * lse
-        drain(u_all.at[it, pl.ds(0, cols - 1)], u_sem.at[it, 1])
+            block_top[pl.ds(0, cols * 2), :] = lse
+            for part in range(2):
+                own = block_top[pl.ds(2 * col + part, 1), :]
+                f_out[part : part + 1, :] = 0.5 * x_square[part : part + 1, :] - (0.25 * LN2) * own
 
         def g_tile(t):
-            line, part = row_id(t) // 2, row_id(t) % 2
-            reduce_tile(t, kk[t] + column_of(u_all[it, line, pl.ds(part, 1), :]))
+            reduce_tile(t, kk[t] + column_of(u_all[pl.ds(row_id(t), 1), :]))
 
         loop(g_tile, UNROLL)
         spread(combine(col_id, rows * 2), g_send.at[it])
@@ -361,15 +366,17 @@
             pltpu.VMEM((cols * 2, BLOCK, width), jnp.bfloat16),
             pltpu.VMEM((rows * 2, BLOCK, width), jnp.bfloat16),
             pltpu.VMEM((ITERS, rows, 2, BLOCK), F32),
-            pltpu.VMEM((ITERS, cols, 2, BLOCK), F32),
+            pltpu.VMEM((cols * 2, BLOCK), F32),
+            pltpu.VMEM((cols, 2, BLOCK), F32),
+            pltpu.VMEM((cols * 2, BLOCK), F32),
             pltpu.VMEM((tiles, BLOCK, BLOCK), F32),
             pltpu.VMEM((tiles, BLOCK, BLOCK), F32),
             pltpu.VMEM((tiles, BLOCK), F32),
             pltpu.VMEM((tiles, BLOCK), F32),
             pltpu.VMEM((tiles, BLOCK), F32),
             pltpu.VMEM((max(rows, cols) * 2, BLOCK), F32),
-            pltpu.VMEM((ITERS, cols, 2, BLOCK), F32),
-            pltpu.VMEM((ITERS, cols, 2, BLOCK), F32),
+            pltpu.VMEM((ITERS, cols * 2, BLOCK), F32),
+            pltpu.VMEM((ITERS, cols, cols * 2, BLOCK), F32),
             pltpu.VMEM((ITERS, rows, 2, BLOCK), F32),
             pltpu.VMEM((ITERS, rows, 2, BLOCK), F32),
             pltpu.VMEM((2, BLOCK), F32),

time: 103 us -> 98.6 us (0.957)
  Pallas kernels: 100 us -> 95.3 us
    pallas_call x1, Pallas kernels: 100 us -> 95.3 us  [body(): pl.pallas_call(functools.partial(kernel, dims), out_shape=(line, line), i...]
where the time goes in v3:
time: 98.6 us; the launch traced here: 98.4 us
  Pallas kernels  95.3 us (97%)
  local copies, waits for them, and re-layouts  1.86 us (2%)
  between operations  1.3 us (1%)
    pallas_call x1, Pallas kernels, body(): pl.pallas_call(functools.partial(kernel, dims), out_shape=(line, line), i...  95.3 us

profile of v3, /device:TPU:1, one launch (start us, length us, event | category | flops | bytes accessed | tf_op | source)
XLA Modules:
  0.0 98.4 jit_solution(15386097356610704327)
XLA Ops:
  1.3 95.3 %shard_map.86 = (f32[2,128]{1,0:T(2,128)}, f32[2,128]{1,0:T(2,128)}) custom-call(s32[2,48]{1,0:T(2,128)} %bitcast.10, s32[1]{0:T(128)S(6)} %copy.11.count_ref, bf16[2,128,256]{2,1,0:T(8,128)(2,1)} %bitcast.8, bf16[2,128,256]{2,1,0:T(8,128)(2,1)} %bitcast.9, f32[2,128]{1,0:T(2,128)} %bitcast.11, f32[2,128]{1,0:T(2,128)} %bitcast.12, f32[2,128]{1,0:T(2,128)} %bitcast.13), custom_call_target="tpu_custom_call" | custom-call | tf_op jit(solution)/shard_map/pallas_call | solution.py:360
  96.6 0.0 copy-start.1
  96.6 0.7 copy-done.1
  97.2 0.0 copy-start
  97.2 0.6 copy.12
  97.8 0.1 copy-done
  97.9 0.6 copy.13
Async XLA Ops:
  96.6 0.7 copy-start.1
  97.2 0.6 copy-start

commit v4 on v3

--- a/solution.py
+++ b/solution.py
@@ -18,7 +18,7 @@
 TINY = 1e-37
 F32 = jnp.float32
 PIECES = 4
-UNROLL = 8
+UNROLL = 24
 
 
 def kernel(

time: 98.6 us -> 96.1 us (0.975)
  Pallas kernels: 95.3 us -> 92.8 us
    pallas_call x1, Pallas kernels: 95.3 us -> 92.8 us  [body(): pl.pallas_call(functools.partial(kernel, dims), out_shape=(line, line), i...]
where the time goes in v4:
time: 96.1 us; the launch traced here: 96 us
  Pallas kernels  92.8 us (97%)
  local copies, waits for them, and re-layouts  1.86 us (2%)
  between operations  1.3 us (1%)
    pallas_call x1, Pallas kernels, body(): pl.pallas_call(functools.partial(kernel, dims), out_shape=(line, line), i...  92.8 us

profile of v4, /device:TPU:1, one launch (start us, length us, event | category | flops | bytes accessed | tf_op | source)
XLA Modules:
  0.0 96.0 jit_solution(12026332248619094615)
XLA Ops:
  1.3 92.8 %shard_map.86 = (f32[2,128]{1,0:T(2,128)}, f32[2,128]{1,0:T(2,128)}) custom-call(s32[2,48]{1,0:T(2,128)} %bitcast.10, s32[1]{0:T(128)S(6)} %copy.11.count_ref, bf16[2,128,256]{2,1,0:T(8,128)(2,1)} %bitcast.8, bf16[2,128,256]{2,1,0:T(8,128)(2,1)} %bitcast.9, f32[2,128]{1,0:T(2,128)} %bitcast.11, f32[2,128]{1,0:T(2,128)} %bitcast.12, f32[2,128]{1,0:T(2,128)} %bitcast.13), custom_call_target="tpu_custom_call" | custom-call | tf_op jit(solution)/shard_map/pallas_call | solution.py:360
  94.1 0.0 copy-start.1
  94.1 0.7 copy-done.1
  94.8 0.0 copy-start
  94.8 0.6 copy.12
  95.3 0.1 copy-done
  95.4 0.6 copy.13
Async XLA Ops:
  94.1 0.7 copy-start.1
  94.8 0.6 copy-start
